TPU v7x, 128 devices: a whole 4x4x4 slice. The times are simulated.
128 devices in a mesh: seq: 32 (over z, y, core), dp: 4 (over x).
Axes of the slice: x: 4, y: 4, z: 4, core: 2. Of those that a mesh axis runs over, the one named last changes fastest.
Arguments:
- queries: bfloat16 [32768, 2048], P(('dp', 'seq')), parts along dimension 0, may hold values from -5 to 5
- keys: bfloat16 [32768, 128], P(('dp', 'seq')), parts along dimension 0, may hold values from -5 to 5
- values: bfloat16 [32768, 128], P(('dp', 'seq')), parts along dimension 0, may hold values from -5 to 5
- lengths: int32 [128], P('dp'), parts along dimension 0, may hold values from 1 to 2048, 8192 in all
- grad_out: bfloat16 [32768, 2048], P(('dp', 'seq')), parts along dimension 0, may hold values from -5 to 5
Outputs:
- attended: bfloat16 [32768, 2048], P(('dp', 'seq')), parts along dimension 0
- grad_queries: bfloat16 [32768, 2048], P(('dp', 'seq')), parts along dimension 0
- grad_keys: bfloat16 [32768, 128], P(('dp', 'seq')), parts along dimension 0
- grad_values: bfloat16 [32768, 128], P(('dp', 'seq')), parts along dimension 0
There are 4 independent parts, one for each index of `dp`. A program takes and returns all parts, laid end to end along the dimension named above; each array names one. Nothing has to cross between parts.
Inputs may be any that keep to these rules, and one draw needn't show every extreme that they name: The lengths sum to 8192.
All inputs are finite; a program needn't handle non-finite values.
Results may differ from a plain program's by a relative error of at most 0.018.
Values may be sent and summed in bfloat16 or wider, within the bound.
A program may use at most 256 MiB of HBM per device.

v0:
```python
import functools
import math

import jax
import jax.numpy as jnp
from jax import lax
from jax.experimental import pallas as pl
from jax.experimental.pallas import tpu as pltpu
from jax.sharding import PartitionSpec as P

NEG_FILL = -1e30
ROWS_Y = 4
SLOTS = 9


def dot_nt(a, b):
    return lax.dot_general(a, b, (((1,), (1,)), ((), ())), preferred_element_type=jnp.float32)


def dot_nn(a, b):
    return lax.dot_general(a, b, (((1,), (0,)), ((), ())), preferred_element_type=jnp.float32)


def kernel(
    n_seq,
    heads,
    len_ref,
    q_hbm,
    k_hbm,
    v_hbm,
    g_hbm,
    o_hbm,
    dq_hbm,
    gk_ref,
    gv_ref,
    q_ref,
    g_ref,
    qt_ref,
    gt_ref,
    kv,
    s_ref,
    m_ref,
    del_ref,
    dq_acc,
    o_ref,
    ds_ref,
    bias,
    part,
    gs,
    gr,
    in_sem,
    out_sem,
    kv_send,
    kv_recv,
    g_send,
    g_recv,
):
    T, D = gk_ref.shape
    R = T * heads
    half = D
    scale = 1.0 / math.sqrt(D)
    scale2 = scale * math.log2(math.e)
    me = lax.axis_index("seq")
    core = lax.rem(me, 2)
    y = lax.rem(me // 2, ROWS_Y)
    row0 = me - (y * 2 + core)
    partner = row0 + y * 2 + (1 - core)
    z_next = lax.rem(me + 2 * ROWS_Y, n_seq)
    z_prev = lax.rem(me + n_seq - 2 * ROWS_Y, n_seq)

    def y_dev(d):
        return row0 + 2 * lax.rem(y + d, ROWS_Y) + core

    def head_copy(src, dst, h, sem):
        return pltpu.make_async_copy(src.at[:, pl.ds(h * D, D)], dst.at[pl.ds(h * T, T), :], sem)

    k_copy = pltpu.make_async_copy(k_hbm, kv.at[0, 0], in_sem.at[0])
    v_copy = pltpu.make_async_copy(v_hbm, kv.at[0, 1], in_sem.at[1])
    k_copy.start()
    v_copy.start()
    for h in range(heads):
        head_copy(q_hbm, q_ref, h, in_sem.at[2 + h]).start()
    for h in range(heads):
        head_copy(g_hbm, g_ref, h, in_sem.at[2 + heads + h]).start()

    barrier = pltpu.get_barrier_semaphore()
    for dev in (z_next, z_prev, partner, y_dev(1), y_dev(2), y_dev(3)):
        pl.semaphore_signal(
            barrier, inc=1, device_id={"seq": dev}, device_id_type=pl.DeviceIdType.MESH
        )

    def kv_to(src, dst, dev):
        return pltpu.make_async_remote_copy(
            src_ref=kv.at[src],
            dst_ref=kv.at[dst],
            send_sem=kv_send.at[dst],
            recv_sem=kv_recv.at[dst],
            device_id={"seq": dev},
            device_id_type=pl.DeviceIdType.MESH,
        )

    def grad_to(i, dev):
        return pltpu.make_async_remote_copy(
            src_ref=gs.at[i],
            dst_ref=gr.at[i],
            send_sem=g_send.at[i],
            recv_sem=g_recv.at[i],
            device_id={"seq": dev},
            device_id_type=pl.DeviceIdType.MESH,
        )

    k_copy.wait()
    v_copy.wait()
    pl.semaphore_wait(barrier, 6)
    kv_to(0, 1, z_next).start()
    for d in (1, 2, 3):

        @pl.when(y + d < ROWS_Y)
        def _():
            kv_to(0, 1 + d, y_dev(d)).start()

    @pl.when(core == 0)
    def _():
        kv_to(0, 5, partner).start()

    first = me * T
    pos = first + lax.broadcasted_iota(jnp.int32, (T, 128), 0)
    starts = jnp.zeros((T, 128), jnp.int32)
    end = jnp.int32(0)
    for i in range(len_ref.shape[0]):
        end = end + len_ref[i]
        starts = jnp.where(pos >= end, end, starts)
    ds_ref[...] = starts
    m_ref[...] = jnp.full(m_ref.shape, -3e38, jnp.float32)
    dq_acc[...] = jnp.zeros(dq_acc.shape, jnp.float32)
    for h in range(heads):
        head_copy(q_hbm, q_ref, h, in_sem.at[2 + h]).wait()
    for h in range(heads):
        head_copy(g_hbm, g_ref, h, in_sem.at[2 + heads + h]).wait()
    for c in range(4):
        w = R // 4
        qt_ref[:, c * w : (c + 1) * w] = q_ref[c * w : (c + 1) * w, :].T
        gt_ref[:, c * w : (c + 1) * w] = g_ref[c * w : (c + 1) * w, :].T

    def score_slot(slot, carry):
        @pl.when(slot >= 1)
        def _():
            kv_to(0, slot, me).wait_recv()

        @pl.when(slot == 1)
        def _():
            for d in (1, 2, 3):

                @pl.when(y + d >= ROWS_Y)
                def _():
                    kv_to(1, 1 + d, y_dev(d)).start()

            @pl.when(core == 1)
            def _():
                kv_to(1, 5, partner).start()

        @pl.when((slot >= 2) & (slot <= 4))
        def _():
            kv_to(slot, slot + 4, partner).start()

        same = jnp.where(slot == 1, 2 * ROWS_Y, 2 * (slot - 1))
        same = jnp.where(slot == 0, 0, same)
        other = jnp.where(core == 1, 2 * (slot - 5) + 1, 2 * (slot - 5) - 1)
        other = jnp.where((slot == 5) & (core == 0), 2 * ROWS_Y - 1, other)
        offset = jnp.where(slot >= 5, other, same)
        base = (me - offset) * T
        lo = ds_ref[...] - base
        hi = offset * T + lax.broadcasted_iota(jnp.int32, (T, 128), 0)
        col = lax.broadcasted_iota(jnp.int32, (T, 128), 1)
        for j in range(T // 128):
            cj = col + j * 128
            bias[:, j * 128 : (j + 1) * 128] = jnp.where(
                (cj >= lo) & (cj <= hi), 0.0, NEG_FILL
            )
        s = dot_nt(q_ref[...], kv[slot, 0]) * scale2
        for h in range(heads):
            rs = slice(h * T, (h + 1) * T)
            sh = s[rs] + bias[...]
            s_ref[slot, rs, :] = sh
            top = m_ref[rs, :]
            for j in range(T // 128):
                top = jnp.maximum(top, sh[:, j * 128 : (j + 1) * 128])
            m_ref[rs, :] = top
        return carry

    lax.fori_loop(0, SLOTS, score_slot, 0)

    per = 4

    def out_chunk(c, carry):
        for u in range(per):
            rs = pl.ds(pl.multiple_of((c * per + u) * T, T), T)
            m = jnp.max(m_ref[rs, :], axis=1, keepdims=True)
            total = jnp.zeros((T, 128), jnp.float32)
            acc = jnp.zeros((T, D), jnp.float32)
            for slot in range(SLOTS):
                p = jnp.exp2(s_ref[slot, rs, :] - m)
                for j in range(T // 128):
                    total = total + p[:, j * 128 : (j + 1) * 128]
                acc = acc + dot_nn(p.astype(jnp.bfloat16), kv[slot, 1])
            total = jnp.sum(total, axis=1, keepdims=True)
            out = (acc / total).astype(jnp.bfloat16)
            o_ref[rs, :] = out
            m_ref[rs, :] = jnp.broadcast_to(m + jnp.log2(total), (T, 128))
            delta = jnp.sum(
                g_ref[rs, :].astype(jnp.float32) * out.astype(jnp.float32), axis=1, keepdims=True
            )
            del_ref[rs, :] = jnp.broadcast_to(delta, (T, 128))
        return carry

    lax.fori_loop(0, heads // per, out_chunk, 0)

    def out_copy(src, dst, h, sem):
        return pltpu.make_async_copy(src.at[pl.ds(h * T, T), :], dst.at[:, pl.ds(h * D, D)], sem)

    for h in range(heads):
        out_copy(o_ref, o_hbm, h, out_sem.at[h]).start()

    def back_slot(i, carry):
        slot = jnp.where(i < 3, 6 + i, jnp.where(i < 6, i - 1, jnp.where(i == 6, 5, 8 - i)))
        kk = kv[slot, 0]
        vv = kv[slot, 1]
        dk = jnp.zeros((D, T), jnp.float32)
        dv = jnp.zeros((D, T), jnp.float32)
        step = 2 * T
        for b in range(R // step):
            rs = slice(b * step, (b + 1) * step)
            dp = dot_nt(g_ref[rs, :], vv)
            lse = m_ref[rs, :]
            delta = del_ref[rs, :]
            p = jnp.exp2(s_ref[slot, rs, :] - jnp.concatenate([lse, lse], axis=1))
            pb = p.astype(jnp.bfloat16)
            dsb = (p * (dp - jnp.concatenate([delta, delta], axis=1))).astype(jnp.bfloat16)
            dq_acc[rs, :] += dot_nn(dsb, kk)
            dv = dv + dot_nn(gt_ref[:, rs], pb)
            dk = dk + dot_nn(qt_ref[:, rs], dsb)
        part[0] = dk
        part[1] = dv

        @pl.when(i < 3)
        def _():
            gs[i] = part[...].astype(jnp.bfloat16)
            grad_to(i, partner).start()

        @pl.when((i >= 3) & (i < 6))
        def _():
            grad_to(i - 3, me).wait_recv()
            gs[i] = (part[...] + gr[i - 3].astype(jnp.float32)).astype(jnp.bfloat16)
            grad_to(i, row0 + 2 * lax.rem(y + 6 - i, ROWS_Y) + core).start()

        @pl.when(i == 6)
        def _():
            gs[6] = part[...].astype(jnp.bfloat16)
            grad_to(6, partner).start()

        @pl.when(i == 7)
        def _():
            total = part[...]
            for j in (3, 4, 5, 6):
                grad_to(j, me).wait_recv()
                mine = (y + (j - 2) >= ROWS_Y) if j < 6 else (core == 1)
                total = total + jnp.where(mine, gr[j].astype(jnp.float32), 0.0)
            gs[7] = total.astype(jnp.bfloat16)
            grad_to(7, z_prev).start()

        return carry

    lax.fori_loop(0, SLOTS, back_slot, 0)

    q_ref[...] = (dq_acc[...] * scale).astype(jnp.bfloat16)
    for h in range(heads):
        out_copy(q_ref, dq_hbm, h, out_sem.at[heads + h]).start()

    total = part[...]
    for j in (3, 4, 5, 6):
        mine = (y + (j - 2) < ROWS_Y) if j < 6 else (core == 0)
        total = total + jnp.where(mine, gr[j].astype(jnp.float32), 0.0)
    grad_to(7, me).wait_recv()
    total = total + gr[7].astype(jnp.float32)
    gk_ref[...] = (total[0] * scale).T.astype(jnp.bfloat16)
    gv_ref[...] = total[1].T.astype(jnp.bfloat16)

    for j in range(8):
        kv_to(0, 1 + j, me).wait_send()
        grad_to(j, me).wait_send()
    for h in range(heads):
        out_copy(o_ref, o_hbm, h, out_sem.at[h]).wait()
        out_copy(q_ref, dq_hbm, h, out_sem.at[heads + h]).wait()


def solution(mesh):
    n_seq = mesh.shape["seq"]

    def shards(queries, keys, values, lengths, grad_out):
        T, D = keys.shape
        heads = queries.shape[1] // D
        R = T * heads
        f32, bf16 = jnp.float32, jnp.bfloat16
        hbm = pl.BlockSpec(memory_space=pl.ANY)
        vmem = pl.BlockSpec(memory_space=pltpu.VMEM)
        smem = pl.BlockSpec(memory_space=pltpu.SMEM)
        dma = pltpu.SemaphoreType.DMA
        return pl.pallas_call(
            functools.partial(kernel, n_seq, heads),
            out_shape=(
                jax.ShapeDtypeStruct(queries.shape, bf16),
                jax.ShapeDtypeStruct(queries.shape, bf16),
                jax.ShapeDtypeStruct(keys.shape, bf16),
                jax.ShapeDtypeStruct(values.shape, bf16),
            ),
            in_specs=[smem, hbm, hbm, hbm, hbm],
            out_specs=(hbm, hbm, vmem, vmem),
            scratch_shapes=[
                pltpu.VMEM((R, D), bf16),
                pltpu.VMEM((R, D), bf16),
                pltpu.VMEM((D, R), bf16),
                pltpu.VMEM((D, R), bf16),
                pltpu.VMEM((SLOTS, 2, T, D), bf16),
                pltpu.VMEM((SLOTS, R, T), f32),
                pltpu.VMEM((R, 128), f32),
                pltpu.VMEM((R, 128), f32),
                pltpu.VMEM((R, D), f32),
                pltpu.VMEM((R, D), bf16),
                pltpu.VMEM((T, 128), jnp.int32),
                pltpu.VMEM((T, T), f32),
                pltpu.VMEM((2, D, T), f32),
                pltpu.VMEM((8, 2, D, T), bf16),
                pltpu.VMEM((8, 2, D, T), bf16),
                dma((2 + 2 * heads,)),
                dma((2 * heads,)),
                dma((SLOTS,)),
                dma((SLOTS,)),
                dma((8,)),
                dma((8,)),
            ],
            compiler_params=pltpu.CompilerParams(
                collective_id=0, has_side_effects=True, vmem_limit_bytes=67043328
            ),
        )(lengths, queries, keys, values, grad_out)

    spec = P(("dp", "seq"), None)
    return jax.shard_map(
        shards,
        mesh=mesh,
        in_specs=(spec, spec, spec, P("dp"), spec),
        out_specs=(spec, spec, spec, spec),
        check_vma=False,
    )
```

profile of v0, /device:TPU:10, one launch (start us, length us, event | category | flops | bytes accessed | tf_op | source)
XLA Modules:
  0.0 60.9 jit_solution(1352349677883893149)
XLA Ops:
  0.6 55.3 %shard_map.84 = (bf16[256,2048]{1,0:T(8,128)(2,1)}, bf16[256,2048]{1,0:T(8,128)(2,1)}, bf16[256,128]{1,0:T(8,128)(2,1)}, bf16[256,128]{1,0:T(8,128)(2,1)}) custom-call(s32[32]{0:T(128)} %len_ref.1, bf16[256,2048]{1,0:T(8,128)(2,1)} %q_hbm.1, bf16[256,128]{1,0:T(8,128)(2,1)} %k_hbm.1, bf16[256,128]{1,0:T(8,128)(2,1)} %v_hbm.1, bf16[256,2048]{1,0:T(8,128)(2,1)} %g_hbm.1), custom_call_target="tpu_custom_call" | custom-call | tf_op jit(solution)/shard_map/pallas_call | solution.py:308
  56.0 0.0 copy-start
  56.0 2.4 %copy.13 = bf16[256,2048]{1,0:T(8,128)(2,1)} copy(bf16[256,2048]{1,0:T(8,128)(2,1)} %get-tuple-element.8) | data formatting | bytes 2097152
  58.4 0.0 copy-done
  58.4 0.0 copy-start.2
  58.4 1.0 %copy.14 = bf16[256,2048]{1,0:T(8,128)(2,1)} copy(bf16[256,2048]{1,0:T(8,128)(2,1)S(1)} %copy-done) | data formatting | bytes 2097152
  59.4 0.0 copy-done.2
  59.4 0.0 copy-start.1
  59.4 0.6 %copy.15 = bf16[256,128]{1,0:T(8,128)(2,1)} copy(bf16[256,128]{1,0:T(8,128)(2,1)S(1)} %copy-done.2) | data formatting | bytes 131072
  60.0 0.2 copy-done.1
  60.2 0.6 %copy.16 = bf16[256,128]{1,0:T(8,128)(2,1)} copy(bf16[256,128]{1,0:T(8,128)(2,1)S(1)} %copy-done.1) | data formatting | bytes 131072
Async XLA Ops:
  56.0 2.4 %copy-start = (bf16[256,2048]{1,0:T(8,128)(2,1)S(1)}, bf16[256,2048]{1,0:T(8,128)(2,1)}, u32[]{:S(2)}) copy-start(bf16[256,2048]{1,0:T(8,128)(2,1)} %get-tuple-element.9) | copy-start | bytes 3145732
  58.4 1.0 %copy-start.2 = (bf16[256,128]{1,0:T(8,128)(2,1)S(1)}, bf16[256,128]{1,0:T(8,128)(2,1)}, u32[]{:S(2)}) copy-start(bf16[256,128]{1,0:T(8,128)(2,1)} %get-tuple-element.10) | copy-start | bytes 196612
  59.4 0.9 %copy-start.1 = (bf16[256,128]{1,0:T(8,128)(2,1)S(1)}, bf16[256,128]{1,0:T(8,128)(2,1)}, u32[]{:S(2)}) copy-start(bf16[256,128]{1,0:T(8,128)(2,1)} %get-tuple-element.11) | copy-start | bytes 196612
where the time goes:
time: 61.1 us; the launch traced here: 60.9 us
  Pallas kernels  55.3 us (91%)
  local copies, waits for them, and re-layouts  4.86 us (8%)
  between operations  0.65 us (1%)
    pallas_call x1, Pallas kernels, shards(): pl.pallas_call(functools.partial(kernel, n_seq, heads), out_shape=(jax.Sh...  55.3 us
    unnamed x10, local copies, waits for them, and re-layouts  4.86 us

commit v1 on v0

--- a/solution.py
+++ b/solution.py
@@ -89,12 +89,12 @@
             barrier, inc=1, device_id={"seq": dev}, device_id_type=pl.DeviceIdType.MESH
         )
 
-    def kv_to(src, dst, dev):
+    def kv_to(which, src, dst, dev):
         return pltpu.make_async_remote_copy(
-            src_ref=kv.at[src],
-            dst_ref=kv.at[dst],
-            send_sem=kv_send.at[dst],
-            recv_sem=kv_recv.at[dst],
+            src_ref=kv.at[src, which],
+            dst_ref=kv.at[dst, which],
+            send_sem=kv_send.at[which, dst],
+            recv_sem=kv_recv.at[which, dst],
             device_id={"seq": dev},
             device_id_type=pl.DeviceIdType.MESH,
         )
@@ -109,19 +109,30 @@
             device_id_type=pl.DeviceIdType.MESH,
         )
 
-    k_copy.wait()
-    v_copy.wait()
-    pl.semaphore_wait(barrier, 6)
-    kv_to(0, 1, z_next).start()
-    for d in (1, 2, 3):
-
-        @pl.when(y + d < ROWS_Y)
-        def _():
-            kv_to(0, 1 + d, y_dev(d)).start()
-
-    @pl.when(core == 0)
-    def _():
-        kv_to(0, 5, partner).start()
+    def own_to_row(which):
+        for d in (1, 2, 3):
+
+            @pl.when(y + d < ROWS_Y)
+            def _():
+                kv_to(which, 0, 2 + d, y_dev(d)).start()
+
+        @pl.when(core == 0)
+        def _():
+            kv_to(which, 0, 2, partner).start()
+
+    def back_to_row(which):
+        for d in (1, 2, 3):
+
+            @pl.when(y + d >= ROWS_Y)
+            def _():
+                kv_to(which, 1, 2 + d, y_dev(d)).start()
+
+        @pl.when(core == 1)
+        def _():
+            kv_to(which, 1, 2, partner).start()
+
+    def kv_wait(which, slot):
+        kv_to(which, 0, slot, me).wait_recv()
 
     first = me * T
     pos = first + lax.broadcasted_iota(jnp.int32, (T, 128), 0)
@@ -132,42 +143,56 @@
         starts = jnp.where(pos >= end, end, starts)
     ds_ref[...] = starts
     m_ref[...] = jnp.full(m_ref.shape, -3e38, jnp.float32)
-    dq_acc[...] = jnp.zeros(dq_acc.shape, jnp.float32)
+
+    k_copy.wait()
+    v_copy.wait()
+    pl.semaphore_wait(barrier, 6)
+    kv_to(0, 0, 1, z_next).start()
+    own_to_row(0)
+    kv_to(1, 0, 1, z_next).start()
     for h in range(heads):
         head_copy(q_hbm, q_ref, h, in_sem.at[2 + h]).wait()
-    for h in range(heads):
-        head_copy(g_hbm, g_ref, h, in_sem.at[2 + heads + h]).wait()
-    for c in range(4):
-        w = R // 4
-        qt_ref[:, c * w : (c + 1) * w] = q_ref[c * w : (c + 1) * w, :].T
-        gt_ref[:, c * w : (c + 1) * w] = g_ref[c * w : (c + 1) * w, :].T
 
     def score_slot(slot, carry):
+        @pl.when(slot == 1)
+        def _():
+            dq_acc[...] = jnp.zeros(dq_acc.shape, jnp.float32)
+            for h in range(heads):
+                head_copy(g_hbm, g_ref, h, in_sem.at[2 + heads + h]).wait()
+            w = R // 4
+            for c in range(4):
+                qt_ref[:, c * w : (c + 1) * w] = q_ref[c * w : (c + 1) * w, :].T
+                gt_ref[:, c * w : (c + 1) * w] = g_ref[c * w : (c + 1) * w, :].T
+
         @pl.when(slot >= 1)
         def _():
-            kv_to(0, slot, me).wait_recv()
+            kv_wait(0, slot)
 
         @pl.when(slot == 1)
         def _():
-            for d in (1, 2, 3):
-
-                @pl.when(y + d >= ROWS_Y)
-                def _():
-                    kv_to(1, 1 + d, y_dev(d)).start()
-
-            @pl.when(core == 1)
-            def _():
-                kv_to(1, 5, partner).start()
-
-        @pl.when((slot >= 2) & (slot <= 4))
-        def _():
-            kv_to(slot, slot + 4, partner).start()
-
-        same = jnp.where(slot == 1, 2 * ROWS_Y, 2 * (slot - 1))
+            back_to_row(0)
+            own_to_row(1)
+
+        @pl.when((slot >= 3) & (slot <= 5))
+        def _():
+            kv_to(0, slot, slot + 3, partner).start()
+
+        @pl.when(slot == 3)
+        def _():
+            kv_wait(1, 1)
+            back_to_row(1)
+
+        @pl.when(slot == 8)
+        def _():
+            for j in (3, 4, 5):
+                kv_wait(1, j)
+                kv_to(1, j, j + 3, partner).start()
+
+        same = jnp.where(slot == 1, 2 * ROWS_Y, 2 * (slot - 2))
         same = jnp.where(slot == 0, 0, same)
         other = jnp.where(core == 1, 2 * (slot - 5) + 1, 2 * (slot - 5) - 1)
-        other = jnp.where((slot == 5) & (core == 0), 2 * ROWS_Y - 1, other)
-        offset = jnp.where(slot >= 5, other, same)
+        near = jnp.where(core == 1, 1, 2 * ROWS_Y - 1)
+        offset = jnp.where(slot >= 6, other, jnp.where(slot == 2, near, same))
         base = (me - offset) * T
         lo = ds_ref[...] - base
         hi = offset * T + lax.broadcasted_iota(jnp.int32, (T, 128), 0)
@@ -189,6 +214,9 @@
         return carry
 
     lax.fori_loop(0, SLOTS, score_slot, 0)
+
+    for j in (2, 6, 7, 8):
+        kv_wait(1, j)
 
     per = 4
 
@@ -222,7 +250,7 @@
         out_copy(o_ref, o_hbm, h, out_sem.at[h]).start()
 
     def back_slot(i, carry):
-        slot = jnp.where(i < 3, 6 + i, jnp.where(i < 6, i - 1, jnp.where(i == 6, 5, 8 - i)))
+        slot = jnp.where(i < 3, 6 + i, jnp.where(i < 6, i, 8 - i))
         kk = kv[slot, 0]
         vv = kv[slot, 1]
         dk = jnp.zeros((D, T), jnp.float32)
@@ -286,7 +314,8 @@
     gv_ref[...] = total[1].T.astype(jnp.bfloat16)
 
     for j in range(8):
-        kv_to(0, 1 + j, me).wait_send()
+        kv_to(0, 0, 1 + j, me).wait_send()
+        kv_to(1, 0, 1 + j, me).wait_send()
         grad_to(j, me).wait_send()
     for h in range(heads):
         out_copy(o_ref, o_hbm, h, out_sem.at[h]).wait()
@@ -333,8 +362,8 @@
                 pltpu.VMEM((8, 2, D, T), bf16),
                 dma((2 + 2 * heads,)),
                 dma((2 * heads,)),
-                dma((SLOTS,)),
-                dma((SLOTS,)),
+                dma((2, SLOTS)),
+                dma((2, SLOTS)),
                 dma((8,)),
                 dma((8,)),
             ],

time: 61.1 us -> 60.9 us (level)
  no operation moved by 1% of the time
where the time goes in v1:
time: 60.9 us; the launch traced here: 60.7 us
  Pallas kernels  55.2 us (91%)
  local copies, waits for them, and re-layouts  4.86 us (8%)
  between operations  0.65 us (1%)
    pallas_call x1, Pallas kernels, shards(): pl.pallas_call(functools.partial(kernel, n_seq, heads), out_shape=(jax.Sh...  55.2 us
    unnamed x10, local copies, waits for them, and re-layouts  4.86 us

profile of v1, /device:TPU:10, one launch (start us, length us, event | category | flops | bytes accessed | tf_op | source)
XLA Modules:
  0.0 60.7 jit_solution(7616385584404169049)
XLA Ops:
  0.6 55.2 %shard_map.84 = (bf16[256,2048]{1,0:T(8,128)(2,1)}, bf16[256,2048]{1,0:T(8,128)(2,1)}, bf16[256,128]{1,0:T(8,128)(2,1)}, bf16[256,128]{1,0:T(8,128)(2,1)}) custom-call(s32[32]{0:T(128)} %len_ref.1, bf16[256,2048]{1,0:T(8,128)(2,1)} %q_hbm.1, bf16[256,128]{1,0:T(8,128)(2,1)} %k_hbm.1, bf16[256,128]{1,0:T(8,128)(2,1)} %v_hbm.1, bf16[256,2048]{1,0:T(8,128)(2,1)} %g_hbm.1), custom_call_target="tpu_custom_call" | custom-call | tf_op jit(solution)/shard_map/pallas_call | solution.py:337
  55.8 0.0 copy-start
  55.8 2.4 %copy.13 = bf16[256,2048]{1,0:T(8,128)(2,1)} copy(bf16[256,2048]{1,0:T(8,128)(2,1)} %get-tuple-element.8) | data formatting | bytes 2097152
  58.2 0.0 copy-done
  58.2 0.0 copy-start.2
  58.2 1.0 %copy.14 = bf16[256,2048]{1,0:T(8,128)(2,1)} copy(bf16[256,2048]{1,0:T(8,128)(2,1)S(1)} %copy-done) | data formatting | bytes 2097152
  59.2 0.0 copy-done.2
  59.2 0.0 copy-start.1
  59.2 0.6 %copy.15 = bf16[256,128]{1,0:T(8,128)(2,1)} copy(bf16[256,128]{1,0:T(8,128)(2,1)S(1)} %copy-done.2) | data formatting | bytes 131072
  59.8 0.2 copy-done.1
  60.0 0.6 %copy.16 = bf16[256,128]{1,0:T(8,128)(2,1)} copy(bf16[256,128]{1,0:T(8,128)(2,1)S(1)} %copy-done.1) | data formatting | bytes 131072
Async XLA Ops:
  55.8 2.4 %copy-start = (bf16[256,2048]{1,0:T(8,128)(2,1)S(1)}, bf16[256,2048]{1,0:T(8,128)(2,1)}, u32[]{:S(2)}) copy-start(bf16[256,2048]{1,0:T(8,128)(2,1)} %get-tuple-element.9) | copy-start | bytes 3145732
  58.2 1.0 %copy-start.2 = (bf16[256,128]{1,0:T(8,128)(2,1)S(1)}, bf16[256,128]{1,0:T(8,128)(2,1)}, u32[]{:S(2)}) copy-start(bf16[256,128]{1,0:T(8,128)(2,1)} %get-tuple-element.10) | copy-start | bytes 196612
  59.2 0.9 %copy-start.1 = (bf16[256,128]{1,0:T(8,128)(2,1)S(1)}, bf16[256,128]{1,0:T(8,128)(2,1)}, u32[]{:S(2)}) copy-start(bf16[256,128]{1,0:T(8,128)(2,1)} %get-tuple-element.11) | copy-start | bytes 196612
